TPU v7x, 32 devices: a whole 2x2x4 slice. The times are simulated.
32 devices in a mesh: batch: 4 (over z), seq: 2 (over core), ch: 4 (over y, x).
Axes of the slice: x: 2, y: 2, z: 4, core: 2. Of those that a mesh axis runs over, the one named last changes fastest.
Arguments:
- inputs: bfloat16 [16, 1280, 2048], P('batch', 'ch', 'seq'), may hold values from -6 to 6
- segment_ids: int32 [16, 2048], P('batch', 'seq'), may hold values from 0 to 7, never falling along the last dimension, each value on 1 to 512 neighbouring positions
- norm0_gain: float32 [1280], P('ch'), may hold values from 0.1 to 1.9
- norm0_shift: float32 [1280], P('ch'), may hold values from -3 to 3
- w_inner: bfloat16 [1280, 640], P('ch'), may hold values from -0.15625 to 0.15625
- b_inner: float32 [640], P('ch'), may hold values from -3 to 3
- norm1_gain: float32 [640], P('ch'), may hold values from 0.1 to 1.9
- norm1_shift: float32 [640], P('ch'), may hold values from -3 to 3
- w_conv: bfloat16 [5, 640, 640], P(None, 'ch'), may hold values from -0.109375 to 0.109375
- b_conv: float32 [640], P('ch'), may hold values from -3 to 3
- norm2_gain: float32 [640], P('ch'), may hold values from 0.1 to 1.9
- norm2_shift: float32 [640], P('ch'), may hold values from -3 to 3
- w_outer: bfloat16 [640, 1280], P('ch'), may hold values from -0.25 to 0.25
- b_outer: float32 [1280], P('ch'), may hold values from -3 to 3
- cotangent: bfloat16 [16, 1280, 2048], P('batch', 'ch', 'seq'), may hold values from -6 to 6
Outputs:
- output: bfloat16 [16, 1280, 2048], P('batch', 'ch', 'seq')
- input_grad: bfloat16 [16, 1280, 2048], P('batch', 'ch', 'seq')
- grad_norm0_gain: float32 [1280], P('ch')
- grad_norm0_shift: float32 [1280], P('ch')
- grad_w_inner: float32 [1280, 640], P('ch')
- grad_b_inner: float32 [640], P('ch')
- grad_norm1_gain: float32 [640], P('ch')
- grad_norm1_shift: float32 [640], P('ch')
- grad_w_conv: float32 [5, 640, 640], P(None, 'ch')
- grad_b_conv: float32 [640], P('ch')
- grad_norm2_gain: float32 [640], P('ch')
- grad_norm2_shift: float32 [640], P('ch')
- grad_w_outer: float32 [640, 1280], P('ch')
- grad_b_outer: float32 [1280], P('ch')
Inputs may be any that keep to these rules, and one draw needn't show every extreme that they name: `segment_ids`: along a row the ids never fall; each protein is one run of 1 to 512 residues, one run of each row has exactly 512, and every row holds all 8 ids.
All inputs are finite; a program needn't handle non-finite values.
Results may differ from a plain program's by a relative error of at most 0.0065.
Values may be sent and summed in bfloat16 or wider, within the bound.
A program may use at most 192 MiB of HBM per device.

v0:
```python
import jax
import jax.numpy as jnp
from jax import lax
from jax.sharding import PartitionSpec as P

KERNEL_TAPS = 5
DILATION_SPACING = 32
EPSILON = 1e-05


def gelu_exact(values):
    return jax.nn.gelu(values, approximate=False)


def gelu_back(point, grad):
    return jax.vjp(gelu_exact, point)[1](grad)[0]


def normalize(values, gain, shift):
    center = jnp.mean(values, axis=1, keepdims=True)
    offset = values - center
    spread = jnp.mean(offset * offset, axis=1, keepdims=True)
    scale = lax.rsqrt(spread + EPSILON)
    unit = offset * scale
    return (unit * gain[:, None] + shift[:, None], unit, scale)


def normalize_back(grad, unit, scale, gain):
    scaled = grad * gain[:, None]
    first = jnp.mean(scaled, axis=1, keepdims=True)
    second = jnp.mean(scaled * unit, axis=1, keepdims=True)
    return scale * (scaled - first - unit * second)


def neighbour_pairs(seqs, nch, q_count):
    pairs = []
    for s in range(seqs):
        for c in range(nch):
            q = c % q_count
            if q < q_count - 1:
                pairs.append((s * nch + c, s * nch + c + 1))
            elif s < seqs - 1:
                pairs.append((s * nch + c, (s + 1) * nch + c - (q_count - 1)))
    return pairs


def extended(x, width, pairs):
    down = [(j, i) for i, j in pairs]
    length = x.shape[-1]
    before = lax.ppermute(x[..., length - width :], ("seq", "ch"), pairs)
    after = lax.ppermute(x[..., :width], ("seq", "ch"), down)
    return jnp.concatenate([before, x, after], axis=-1)


def shifted_taps(wide, wide_ids, own_ids, offsets, border):
    length = own_ids.shape[-1]
    pieces = []
    for offset in offsets:
        lower = border + offset
        shifted = wide[:, :, lower : lower + length]
        matching = wide_ids[:, lower : lower + length] == own_ids
        pieces.append(jnp.where(matching[:, None, :], shifted, jnp.zeros_like(shifted)))
    return jnp.concatenate(pieces, axis=1)


def to_positions(x, nch, q_count):
    rows, width, length = x.shape
    if q_count > 1:
        x = x.reshape(rows, width, q_count, length // q_count).transpose(0, 2, 1, 3)
        x = x.reshape(rows * q_count, width, length // q_count)
    return lax.all_to_all(x, "ch", 0, 1, tiled=True)


def to_channels(x, nch, q_count, rows):
    x = lax.all_to_all(x, "ch", 1, 0, tiled=True)
    if q_count > 1:
        _, width, part = x.shape
        x = (
            x.reshape(rows, q_count, width, part)
            .transpose(0, 2, 1, 3)
            .reshape(rows, width, q_count * part)
        )
    return x


def local(
    inputs,
    segment_ids,
    norm0_gain,
    norm0_shift,
    w_inner,
    b_inner,
    norm1_gain,
    norm1_shift,
    w_conv,
    b_conv,
    norm2_gain,
    norm2_shift,
    w_outer,
    b_outer,
    cotangent,
):
    nch = lax.axis_size("ch")
    seqs = lax.axis_size("seq")
    batches = lax.axis_size("batch")
    rows, dloc, length = inputs.shape
    hloc = w_conv.shape[1]
    hid = hloc * nch
    dim = dloc * nch
    if rows % nch == 0:
        q_count = 1
    else:
        q_count = nch // rows
    part = length // q_count
    border = 2 * DILATION_SPACING
    offsets = [(k - KERNEL_TAPS // 2) * DILATION_SPACING for k in range(KERNEL_TAPS)]
    back_offsets = [-o for o in offsets]
    pairs = neighbour_pairs(seqs, nch, q_count)
    me = lax.axis_index("ch")
    smalls = [
        norm0_gain,
        norm0_shift,
        b_inner,
        norm1_gain,
        norm1_shift,
        b_conv,
        norm2_gain,
        norm2_shift,
        b_outer,
    ]
    small_all = lax.all_gather(jnp.concatenate(smalls), "ch", axis=0, tiled=False)
    cut = 0
    full = []
    for s in smalls:
        n = s.shape[0]
        full.append(small_all[:, cut : cut + n].reshape(n * nch))
        cut += n
    g0, s0, b_in, g1, s1, b_cv, g2, s2, b_out = full
    packed = jnp.concatenate([w_inner.reshape(-1), w_conv.reshape(-1), w_outer.reshape(-1)])
    packed_all = lax.all_gather(packed.reshape(1, -1, 128), "ch", axis=0, tiled=True).reshape(
        nch, -1
    )
    n_in, n_cv = (w_inner.size, w_conv.size)
    w_in = packed_all[:, :n_in].reshape(dim, hid)
    w_cv = (
        packed_all[:, n_in : n_in + n_cv]
        .reshape(nch, KERNEL_TAPS, hloc, hid)
        .transpose(1, 0, 2, 3)
        .reshape(KERNEL_TAPS, hid, hid)
    )
    w_out = packed_all[:, n_in + n_cv :].reshape(hid, dim)
    x = to_positions(inputs, nch, q_count)
    cot = to_positions(cotangent, nch, q_count)
    prow = x.shape[0]
    if q_count == 1:
        ids = lax.dynamic_slice_in_dim(segment_ids, me * prow, prow, axis=0)
    else:
        ids = lax.dynamic_slice_in_dim(segment_ids, me // q_count, 1, axis=0)
        ids = lax.dynamic_slice_in_dim(ids, me % q_count * part, part, axis=1)
    own_ids = ids + 1
    wide_ids = extended(own_ids, border, pairs)
    residual = x.astype(jnp.float32)
    normed0, unit0, scale0 = normalize(residual, g0, s0)
    hidden0 = gelu_exact(normed0).astype(jnp.bfloat16)
    inner = (
        jnp.einsum("dh,rdl->rhl", w_in, hidden0, preferred_element_type=jnp.float32) + b_in[:, None]
    )
    normed1, unit1, scale1 = normalize(inner, g1, s1)
    hidden1 = gelu_exact(normed1).astype(jnp.bfloat16)
    wide_hidden = extended(hidden1, border, pairs)
    taps = shifted_taps(wide_hidden, wide_ids, own_ids, offsets, border)
    kernel_flat = w_cv.reshape(KERNEL_TAPS * hid, hid)
    mixed = (
        jnp.einsum("co,rcl->rol", kernel_flat, taps, preferred_element_type=jnp.float32)
        + b_cv[:, None]
    )
    normed2, unit2, scale2 = normalize(mixed, g2, s2)
    hidden2 = gelu_exact(normed2).astype(jnp.bfloat16)
    branch = jnp.einsum("hd,rhl->rdl", w_out, hidden2, preferred_element_type=jnp.float32)
    output = (residual + branch + b_out[:, None]).astype(jnp.bfloat16)
    grad_b_outer = jnp.sum(cot.astype(jnp.float32), axis=(0, 2))
    grad_w_outer = jnp.einsum("rhl,rdl->hd", hidden2, cot, preferred_element_type=jnp.float32)
    grad_hidden2 = jnp.einsum("hd,rdl->rhl", w_out, cot, preferred_element_type=jnp.float32)
    grad_normed2 = gelu_back(normed2, grad_hidden2)
    grad_norm2_gain = jnp.sum(grad_normed2 * unit2, axis=(0, 2))
    grad_norm2_shift = jnp.sum(grad_normed2, axis=(0, 2))
    grad_mixed = normalize_back(grad_normed2, unit2, scale2, g2).astype(jnp.bfloat16)
    grad_b_conv = jnp.sum(grad_mixed.astype(jnp.float32), axis=(0, 2))
    grad_w_conv = jnp.einsum(
        "rcl,rol->co", taps, grad_mixed, preferred_element_type=jnp.float32
    ).reshape(KERNEL_TAPS, hid, hid)
    wide_grad = extended(grad_mixed, border, pairs)
    back_taps = shifted_taps(wide_grad, wide_ids, own_ids, back_offsets, border)
    kernel_back = jnp.transpose(w_cv, (0, 2, 1)).reshape(KERNEL_TAPS * hid, hid)
    grad_hidden1 = jnp.einsum(
        "oc,rol->rcl", kernel_back, back_taps, preferred_element_type=jnp.float32
    )
    grad_normed1 = gelu_back(normed1, grad_hidden1)
    grad_norm1_gain = jnp.sum(grad_normed1 * unit1, axis=(0, 2))
    grad_norm1_shift = jnp.sum(grad_normed1, axis=(0, 2))
    grad_inner = normalize_back(grad_normed1, unit1, scale1, g1).astype(jnp.bfloat16)
    grad_b_inner = jnp.sum(grad_inner.astype(jnp.float32), axis=(0, 2))
    grad_w_inner = jnp.einsum(
        "rdl,rhl->dh", hidden0, grad_inner, preferred_element_type=jnp.float32
    )
    grad_hidden0 = jnp.einsum("dh,rhl->rdl", w_in, grad_inner, preferred_element_type=jnp.float32)
    grad_normed0 = gelu_back(normed0, grad_hidden0)
    grad_norm0_gain = jnp.sum(grad_normed0 * unit0, axis=(0, 2))
    grad_norm0_shift = jnp.sum(grad_normed0, axis=(0, 2))
    input_grad = (cot.astype(jnp.float32) + normalize_back(grad_normed0, unit0, scale0, g0)).astype(
        jnp.bfloat16
    )
    output = to_channels(output, nch, q_count, rows)
    input_grad = to_channels(input_grad, nch, q_count, rows)
    grads = [
        grad_norm0_gain,
        grad_norm0_shift,
        grad_w_inner,
        grad_b_inner,
        grad_norm1_gain,
        grad_norm1_shift,
        grad_w_conv.transpose(1, 0, 2),
        grad_b_conv,
        grad_norm2_gain,
        grad_norm2_shift,
        grad_w_outer,
        grad_b_outer,
    ]
    flat = [g.reshape(nch, -1) for g in grads]
    sizes = [f.shape[1] for f in flat]
    stack = jnp.concatenate(flat, axis=1)
    total = stack.shape[1]
    lanes = 128
    spread = seqs * batches * 8 * lanes
    padded = -(-total // spread) * spread
    if padded != total:
        stack = jnp.pad(stack, ((0, 0), (0, padded - total)))
    stack = stack.reshape(nch, padded // lanes, lanes)
    stack = lax.psum_scatter(stack, "seq", scatter_dimension=1, tiled=True)
    stack = lax.psum_scatter(stack, "batch", scatter_dimension=1, tiled=True)
    stack = lax.psum_scatter(stack, "ch", scatter_dimension=0, tiled=True)
    stack = lax.all_gather(stack, ("seq", "batch"), axis=1, tiled=True).reshape(padded)[:total]
    shard_shapes = [
        norm0_gain.shape,
        norm0_shift.shape,
        w_inner.shape,
        b_inner.shape,
        norm1_gain.shape,
        norm1_shift.shape,
        (hloc, KERNEL_TAPS, hid),
        b_conv.shape,
        norm2_gain.shape,
        norm2_shift.shape,
        w_outer.shape,
        b_outer.shape,
    ]
    outs = []
    cut = 0
    for n, shape in zip(sizes, shard_shapes):
        outs.append(stack[cut : cut + n].reshape(shape))
        cut += n
    outs[6] = outs[6].transpose(1, 0, 2)
    return (output, input_grad, *outs)


def solution(mesh):
    return jax.shard_map(
        local,
        mesh=mesh,
        in_specs=(
            P("batch", "ch", "seq"),
            P("batch", "seq"),
            P("ch"),
            P("ch"),
            P("ch", None),
            P("ch"),
            P("ch"),
            P("ch"),
            P(None, "ch", None),
            P("ch"),
            P("ch"),
            P("ch"),
            P("ch", None),
            P("ch"),
            P("batch", "ch", "seq"),
        ),
        out_specs=(
            P("batch", "ch", "seq"),
            P("batch", "ch", "seq"),
            P("ch"),
            P("ch"),
            P("ch", None),
            P("ch"),
            P("ch"),
            P("ch"),
            P(None, "ch", None),
            P("ch"),
            P("ch"),
            P("ch"),
            P("ch", None),
            P("ch"),
        ),
        check_vma=False,
    )
```

profile of v0, /device:TPU:0, one launch (start us, length us, event | category | flops | bytes accessed | tf_op | source)
XLA Modules:
  0.0 816.1 jit_solution(5555885793643184578)
XLA Ops:
  10.0 1.8 reshape.1466
  13.4 5.3 all-to-all-start
  22.4 49.7 %all-gather.1 = f32[4,1,1920]{2,1,0:T(1,128)S(1)} all-gather(f32[1,1,1920]{2,1,0:T(1,128)S(1)} %reshape.1500), channel_id=2, replica_groups=mesh['batch'=4,'seq'=2,'ch'=4] {'ch'}, dimensions={0}, use_global_device_ids=true | all-gather | bytes 38400 | tf_op jit(solution)/shard_map/all_gather | solution.py:131
  73.7 4.8 all-to-all-start.2
  81.5 14.8 %fusion.6 = bf16[1,1280,1,1,1,1,1024]{6,1,5,4,3,2,0:T(8,128)(2,1)} fusion(f32[1,1280,1,1,1,1,1024]{6,1,5,4,3,2,0:T(8,128)S(1)} %bitcast.270, f32[1280]{0:T(1024)S(1)} %add.153, f32[1280]{0:T(1024)S(1)} %mul.431, f32[1024]{0:T(1024)S(1)} %add_rsqrt_fusion.2, f32[1024]{0:T(1024)S(1)} %broadcast_multiply_fusion.8), kind=kLoop, calls=%fused_computation.11 | loop fusion | flops 90439680 | bytes 7882752 | tf_op jit(solution)/shard_map/convert_element_type | solution.py:164
  96.3 48.7 %all-gather.5.cloned.1.call-done = bf16[4,7200,128]{2,1,0:T(8,128)(2,1)} async-done(((bf16[1,7200,128]{2,1,0:T(8,128)(2,1)}), bf16[4,7200,128]{2,1,0:T(8,128)(2,1)}) %all-gather.5.cloned.1.call-update) | async-done | bytes 7372816 | tf_op jit(solution)/shard_map/all_gather | solution.py:140
  145.0 26.1 %copy.86 = bf16[1,4,7200,128]{3,1,2,0:T(4,128)(2,1)S(1)} copy(bf16[1,4,7200,128]{3,2,1,0:T(8,128)(2,1)} %bitcast.283) | data formatting | bytes 14745600
  171.1 3.0 copy-done.6
  174.0 2.0 fusion.110
  176.1 2.3 reshape.1470
  178.4 4.5 fusion.72
  183.5 7.3 multiply_convert_fusion.1
  191.8 1.9 collective-permute-start.1
  193.8 2.7 convert_reduce_fusion.3
  196.5 5.9 copy.61
  202.4 3.6 slice.212
  206.6 2.4 copy.60
  208.9 4.1 reshape.1474
  214.3 7.9 copy.66
  222.2 2.9 fusion.90
  226.6 8.0 constant_dynamic-update-slice_fusion
  237.5 9.6 %copy.69 = bf16[1,3200,1024]{2,1,0:T(8,128)(2,1)} copy(bf16[1,3200,1024]{1,2,0:T(8,128)(2,1)} %fusion.97) | data formatting | bytes 13107200 | tf_op jit(solution)/shard_map/concatenate | solution.py:63
  247.0 9.1 %fusion.74 = (f32[1024]{0:T(1024)S(1)}, f32[1024,640]{1,0:T(8,128)S(1)}) fusion(f32[640]{0:T(1024)S(1)} %add.163, bf16[3200,640]{1,0:T(8,128)(2,1)} %bitcast.279, bf16[1,3200,1024]{1,2,0:T(8,128)(2,1)} %fusion.97), kind=kOutput, calls=%fused_computation.146 | convolution fusion | flops 4195613696 | bytes 13277696 | tf_op jit(solution)/shard_map/co,rcl->rol/dot_general | solution.py:174
  256.7 11.8 %fusion.105 = f32[640,1280]{1,0:T(8,128)} fusion(bf16[1280,1024]{1,0:T(8,128)(2,1)} %bitcast.15, f32[640]{0:T(1024)S(1)} %add.167, f32[640]{0:T(1024)S(1)} %mul.451, f32[1024]{0:T(1024)S(1)} %add_rsqrt_fusion, f32[1024]{0:T(1024)S(1)} %broadcast_multiply_fusion.4, f32[640]{0:T(1024)S(1)} %add.163, f32[1024,640]{1,0:T(8,128)S(1)} %get-tuple-element.121), kind=kOutput, calls=%fused_computation.218 | convolution fusion | flops 1723596800 | bytes 8535552 | tf_op jit(solution)/shard_map/rhl,rdl->hd/dot_general | solution.py:182
  268.6 12.4 %fusion.50 = (f32[640]{0:T(1024)S(1)}, f32[1024]{0:T(1024)S(1)}, f32[1024]{0:T(1024)S(1)}, f32[640]{0:T(1024)S(1)}, f32[1,640,1024]{1,2,0:T(8,128)}) fusion(f32[1024]{0:T(1024)S(1)} %add_rsqrt_fusion, f32[1024]{0:T(1024)S(1)} %broadcast_multiply_fusion.4, f32[640]{0:T(1024)S(1)} %add.163, f32[1024,640]{1,0:T(8,128)S(1)} %get-tuple-element.121, ...), kind=kOutput, calls=%fused_computation.93 | convolution fusion | flops 1732113152 | bytes 9531904 | tf_op jit(solution)/shard_map/hd,rdl->rhl/dot_general | solution.py:183
  281.1 3.1 convert_reduce_fusion.1
  284.3 5.2 reshape.1491
  289.5 3.0 collective-permute-start.5
  293.9 7.6 convolution_bitcast_fusion
  301.4 9.7 %copy.71 = f32[640,5,640]{2,1,0:T(8,128)} copy(f32[640,5,640]{2,0,1:T(8,128)S(1)} %convolution_bitcast_fusion) | data formatting | bytes 16384000 | tf_op jit(solution)/shard_map/transpose | solution.py:222
  311.2 12.0 %reshape.1487 = f32[4,512000]{1,0:T(4,128)} reshape(f32[640,5,640]{2,1,0:T(8,128)} %copy.71) | data formatting | bytes 16384000 | tf_op jit(solution)/shard_map/reshape | solution.py:229
  326.9 13.5 %fusion.56 = (f32[640]{0:T(1024)S(1)}, f32[1024]{0:T(1024)S(1)}, f32[1024]{0:T(1024)S(1)}, f32[640]{0:T(1024)S(1)}, f32[1,640,1024]{1,2,0:T(8,128)}) fusion(f32[1024]{0:T(1024)S(1)} %add_rsqrt_fusion.1, f32[1024]{0:T(1024)S(1)} %broadcast_multiply_fusion.5, f32[640]{0:T(1024)S(1)} %add.156, f32[1024,640]{1,0:T(8,128)S(1)} %copy-done.2, f32[640]{0:T(1024)S(1)} %mul.441, ...), kind=kOutput, calls=%fused_computation.104 | convolution fusion | flops 4248695808 | bytes 15921664 | tf_op jit(solution)/shard_map/oc,rol->rcl/dot_general | solution.py:195
  340.5 3.3 convert_reduce_fusion.2
  343.9 6.0 fusion.57
  349.9 3.5 reshape.1482
  353.4 19.2 %multiply_reduce_fusion = (f32[1280]{0:T(1024)S(1)}, f32[1024]{0:T(1024)S(1)}, f32[1024]{0:T(1024)S(1)}, f32[1280]{0:T(1024)S(1)}, f32[1,1280,1024]{1,2,0:T(8,128)}) fusion(f32[1,1280,1024]{1,2,0:T(8,128)} %copy.61, f32[1024]{0:T(1024)S(1)} %copy-done.15, f32[1024]{0:T(1024)S(1)} %copy-done.17, f32[1280]{0:T(1024)S(1)} %copy-done.13, ...), kind=kOutput, calls=%fused_computation.24 | convolution fusion | flops 1785196032 | bytes 13471744 | tf_op jit(solution)/shard_map/dh,rhl->rdl/dot_general | solution.py:206
  375.6 1.8 constant_dynamic-update-slice_fusion.2
  381.6 43.2 %dynamic-update-slice.6 = f32[4,923520]{1,0:T(4,128)} dynamic-update-slice(f32[4,923520]{1,0:T(4,128)} %dynamic-update-slice.5, f32[4,512000]{1,0:T(4,128)} %reshape.1487, s32[]{} %constant.29, s32[]{} %constant.35) | dynamic-update-slice | bytes 16384004
  426.2 1.7 dynamic-update-slice.8
  429.4 17.2 %dynamic-update-slice.10 = f32[4,923520]{1,0:T(4,128)} dynamic-update-slice(f32[4,923520]{1,0:T(4,128)} %dynamic-update-slice.9, f32[4,204800]{1,0:T(4,128)S(1)} %copy-done.7, s32[]{} %constant.29, s32[]{} %constant.146) | dynamic-update-slice | bytes 6553604
  448.0 12.8 %pad_bitcast_fusion = f32[1,4,7232,128]{3,1,2,0:T(4,128)} fusion(f32[4,923520]{1,0:T(4,128)} %dynamic-update-slice.11), kind=kLoop, calls=%fused_computation.1 | loop fusion | bytes 29587456
  460.8 11.4 %copy.85 = f32[1,4,7232,128]{3,2,1,0:T(8,128)} copy(f32[1,4,7232,128]{3,1,2,0:T(4,128)} %pad_bitcast_fusion) | data formatting | bytes 29622272
  472.2 24.9 %reduce-scatter.6.cloned.1.call-done = f32[4,3616,128]{2,1,0:T(8,128)} async-done(((f32[4,7232,128]{2,1,0:T(8,128)}), f32[4,3616,128]{2,1,0:T(8,128)}) %reduce-scatter.6.cloned.1.call-update) | async-done | bytes 7405584 | tf_op jit(solution)/shard_map/reduce_scatter | solution.py:239
  497.2 132.5 %reduce-scatter.8.cloned.1.call-done = f32[4,904,128]{2,1,0:T(8,128)} async-done(((f32[4,3616,128]{2,1,0:T(8,128)}), f32[4,904,128]{2,1,0:T(8,128)}) %reduce-scatter.8.cloned.1.call-update) | async-done | bytes 1851408 | tf_op jit(solution)/shard_map/reduce_scatter | solution.py:240
  629.7 37.5 %reduce-scatter.10.cloned.1.call-done = f32[1,904,128]{2,1,0:T(8,128)} async-done(((f32[4,904,128]{2,1,0:T(8,128)}), f32[1,904,128]{2,1,0:T(8,128)}) %reduce-scatter.10.cloned.1.call-update) | async-done | bytes 462864
  667.3 11.7 %fusion.12 = bf16[1,1280,1024]{1,2,0:T(8,128)(2,1)} fusion(f32[1,1280,1024]{1,2,0:T(8,128)} %copy.61, bf16[640,1280]{1,0:T(8,128)(2,1)} %reshape.1474, f32[1280]{0:T(1024)S(1)} %add.171, f32[640]{0:T(1024)S(1)} %add.167, f32[640]{0:T(1024)S(1)} %mul.451, f32[1024]{0:T(1024)S(1)} %add_rsqrt_fusion, f32[1024]{0:T(1024)S(1)} %broadcast_multiply_fusion.4, ...), kind=kOutput, calls=%fused_computation.18 | convolution fusion | flops 1727528960 | bytes 12145152 | tf_op jit(solution)/shard_map/hd,rhl->rdl/dot_general | solution.py:179
  679.0 11.6 %copy.62 = bf16[1,1280,1024]{2,0,1:T(2,128)(2,1)} copy(bf16[1,1280,1024]{1,2,0:T(8,128)(2,1)} %fusion.12) | data formatting | bytes 5242880 | tf_op jit(solution)/shard_map/convert_element_type | solution.py:180
  691.1 15.6 %reduce.29 = bf16[1280,1024]{1,0:T(8,128)(2,1)S(1)} reduce(bf16[1280,1,1024]{2,1,0:T(2,128)(2,1)} %bitcast.274, bf16[]{:T(256)} %broadcast.2394), dimensions={1}, to_apply=%bitcast.237.reduce_sub_computation | reduce | bytes 5242882
  706.7 3.1 reshape.1509
  709.9 4.6 all-to-all-start.1
  714.4 4.9 copy.67
  719.4 6.4 add_convert_fusion
  725.8 8.3 %copy.68 = bf16[1,1280,1024]{2,0,1:T(2,128)(2,1)} copy(bf16[1,1280,1024]{1,2,0:T(8,128)(2,1)S(1)} %add_convert_fusion) | data formatting | bytes 5242880 | tf_op jit(solution)/shard_map/convert_element_type | solution.py:210
  734.0 15.6 %reduce.30 = bf16[1280,1024]{1,0:T(8,128)(2,1)S(1)} reduce(bf16[1280,1,1024]{2,1,0:T(2,128)(2,1)} %bitcast.275, bf16[]{:T(256)} %broadcast.2394), dimensions={1}, to_apply=%bitcast.239.reduce_sub_computation | reduce | bytes 5242882
  749.6 3.2 reshape.1511
  752.8 4.3 all-to-all-start.3
  757.1 5.5 reshape.1510
  762.7 5.0 copy.77
  767.7 19.7 %all-to-all-done.3 = bf16[4,2,163840]{2,1,0:T(2,128)(2,1)S(1)} async-done(((bf16[4,2,163840]{2,1,0:T(2,128)(2,1)}), bf16[4,2,163840]{2,1,0:T(2,128)(2,1)S(1)}, u32[]{:S(2)}, u32[]{:S(2)}) %all-to-all-start.3) | async-done | bytes 2621472 | tf_op jit(solution)/shard_map/all_to_all | solution.py:75
  787.3 3.8 reshape.1512
  791.2 5.0 copy.78
  796.2 2.3 slice_bitcast_fusion
  800.1 1.9 slice.231
  805.2 2.4 reshape.1494
  (157 shorter events, 45.0 us)
Async XLA Ops:
  7.2 137.8 %all-gather.5.cloned.1.call-start = ((), (), s32[]{:S(2)}) async-start(), calls=%async_computation.7 | async-start | bytes 9216000 | tf_op jit(solution)/shard_map/all_gather | solution.py:140
  13.2 9.0 %copy-start.22 = (f32[320]{0:T(512)S(1)}, f32[320]{0:T(512)}, u32[]{:S(2)}) copy-start(f32[320]{0:T(512)} %param.17) | copy-start | bytes 3844
  13.3 9.0 %copy-start.23 = (f32[320]{0:T(512)S(1)}, f32[320]{0:T(512)}, u32[]{:S(2)}) copy-start(f32[320]{0:T(512)} %param.18) | copy-start | bytes 3844
  13.3 9.0 %copy-start.24 = (f32[320]{0:T(512)S(1)}, f32[320]{0:T(512)}, u32[]{:S(2)}) copy-start(f32[320]{0:T(512)} %param.28) | copy-start | bytes 3844
  13.3 9.0 %copy-start.25 = (f32[160]{0:T(256)S(1)}, f32[160]{0:T(256)}, u32[]{:S(2)}) copy-start(f32[160]{0:T(256)} %param.20) | copy-start | bytes 1924
  13.3 9.0 %copy-start.26 = (f32[160]{0:T(256)S(1)}, f32[160]{0:T(256)}, u32[]{:S(2)}) copy-start(f32[160]{0:T(256)} %param.21) | copy-start | bytes 1924
  13.3 9.0 %copy-start.27 = (f32[160]{0:T(256)S(1)}, f32[160]{0:T(256)}, u32[]{:S(2)}) copy-start(f32[160]{0:T(256)} %param.22) | copy-start | bytes 1924
  13.3 9.0 %copy-start.28 = (f32[160]{0:T(256)S(1)}, f32[160]{0:T(256)}, u32[]{:S(2)}) copy-start(f32[160]{0:T(256)} %param.24) | copy-start | bytes 1924
  13.3 9.0 %copy-start.29 = (f32[160]{0:T(256)S(1)}, f32[160]{0:T(256)}, u32[]{:S(2)}) copy-start(f32[160]{0:T(256)} %param.25) | copy-start | bytes 1924
  13.3 9.0 %copy-start.30 = (f32[160]{0:T(256)S(1)}, f32[160]{0:T(256)}, u32[]{:S(2)}) copy-start(f32[160]{0:T(256)} %param.26) | copy-start | bytes 1924
  13.4 60.4 %all-to-all-start = ((bf16[4,320,1024]{2,1,0:T(8,128)(2,1)}), bf16[4,320,1024]{2,1,0:T(8,128)(2,1)S(1)}, u32[]{:S(2)}, u32[]{:S(2)}) async-start(bf16[4,320,1024]{2,1,0:T(8,128)(2,1)} %param.15), calls=%async_computation | async-start | bytes 5242880 | tf_op jit(solution)/shard_map/all_to_all | solution.py:71
  19.5 54.1 %collective-permute-start = (s32[1,64]{1,0:T(1,128)S(1)}, s32[1,64]{1,0:T(1,128)S(1)}, u32[]{:S(2)}, u32[]{:S(2)}) collective-permute-start(s32[1,64]{1,0:T(1,128)S(1)} %get-tuple-element.116), channel_id=1, source_target_pairs={{0,4},{1,5},{2,6},{3,7},{8,12},{9,13},{10,14},{11,15},{16,20},{17,... | collective-permute-start | bytes 776 | tf_op jit(solution)/shard_map/ppermute | solution.py:50
  20.9 52.6 %collective-permute-start.2 = (s32[1,64]{1,0:T(1,128)S(1)}, s32[1,64]{1,0:T(1,128)S(1)}, u32[]{:S(2)}, u32[]{:S(2)}) collective-permute-start(s32[1,64]{1,0:T(1,128)S(1)} %get-tuple-element.117), channel_id=1, source_target_pairs={{4,0},{5,1},{6,2},{7,3},{12,8},{13,9},{14,10},{15,11},{20,16},{21,... | collective-permute-start | bytes 776 | tf_op jit(solution)/shard_map/ppermute | solution.py:51
  73.1 7.3 copy-start.12
  73.6 6.9 copy-start.18
  73.7 120.1 %all-to-all-start.2 = ((bf16[4,320,1024]{2,1,0:T(8,128)(2,1)}), bf16[4,320,1024]{2,1,0:T(8,128)(2,1)}, u32[]{:S(2)}, u32[]{:S(2)}) async-start(bf16[4,320,1024]{2,1,0:T(8,128)(2,1)} %param.29), calls=%async_computation.2 | async-start | bytes 5242880 | tf_op jit(solution)/shard_map/all_to_all | solution.py:71
  78.5 418.6 %reduce-scatter.6.cloned.1.call-start = ((), (), s32[]{:S(2)}) async-start(), calls=%async_computation.8 | async-start | bytes 22216704 | tf_op jit(solution)/shard_map/reduce_scatter | solution.py:239
  79.2 2.3 copy-start
  79.6 16.6 %copy-start.14 = (f32[1024]{0:T(1024)}, f32[1024]{0:T(1024)S(1)}, u32[]{:S(2)}) copy-start(f32[1024]{0:T(1024)S(1)} %broadcast_multiply_fusion.8) | copy-start | bytes 12292
  80.4 15.9 %copy-start.16 = (f32[1024]{0:T(1024)}, f32[1024]{0:T(1024)S(1)}, u32[]{:S(2)}) copy-start(f32[1024]{0:T(1024)S(1)} %add_rsqrt_fusion.2) | copy-start | bytes 12292
  171.0 3.0 copy-start.6
  182.9 43.6 %copy-start.1 = (f32[1024,640]{1,0:T(8,128)}, f32[1024,640]{1,0:T(8,128)S(1)}, u32[]{:S(2)}) copy-start(f32[1024,640]{1,0:T(8,128)S(1)} %get-tuple-element.119) | copy-start | bytes 7864324
  190.8 1.1 copy-start.4
  191.8 30.4 %collective-permute-start.1 = (bf16[1,640,64]{1,2,0:T(8,128)(2,1)S(1)}, bf16[1,640,64]{1,2,0:T(8,128)(2,1)S(1)}, u32[]{:S(2)}, u32[]{:S(2)}) collective-permute-start(bf16[1,640,64]{1,2,0:T(8,128)(2,1)S(1)} %get-tuple-element.106), channel_id=1, source_target_pairs={{0,4},{1,5},{2,6},{3,7},{8,12},{9,13},{10,14},{11,15},{16,20},{17,... | collective-permute-start | bytes 245768 | tf_op jit(solution)/shard_map/ppermute | solution.py:50
  213.1 21.5 %collective-permute-start.3 = (bf16[1,640,64]{1,2,0:T(8,128)(2,1)S(1)}, bf16[1,640,64]{1,2,0:T(8,128)(2,1)S(1)}, u32[]{:S(2)}, u32[]{:S(2)}) collective-permute-start(bf16[1,640,64]{1,2,0:T(8,128)(2,1)S(1)} %get-tuple-element.105), channel_id=1, source_target_pairs={{4,0},{5,1},{6,2},{7,3},{12,8},{13,9},{14,10},{15,11},{20,16},{21,... | collective-permute-start | bytes 245768 | tf_op jit(solution)/shard_map/ppermute | solution.py:51
  222.2 2.9 copy-start.5
  256.2 12.4 %copy-start.8 = (f32[1024,640]{1,0:T(8,128)}, f32[1024,640]{1,0:T(8,128)S(1)}, u32[]{:S(2)}) copy-start(f32[1024,640]{1,0:T(8,128)S(1)} %get-tuple-element.121) | copy-start | bytes 7864324
  256.7 11.8 %copy-start.11 = (bf16[640,1280]{1,0:T(8,128)(2,1)S(1)}, bf16[640,1280]{1,0:T(8,128)(2,1)}, u32[]{:S(2)}) copy-start(bf16[640,1280]{1,0:T(8,128)(2,1)} %reshape.1474) | copy-start | bytes 4915204
  289.5 34.6 %collective-permute-start.5 = (bf16[1,640,64]{1,2,0:T(8,128)(2,1)S(1)}, bf16[1,640,64]{1,2,0:T(8,128)(2,1)S(1)}, u32[]{:S(2)}, u32[]{:S(2)}) collective-permute-start(bf16[1,640,64]{1,2,0:T(8,128)(2,1)S(1)} %get-tuple-element.103), channel_id=1, source_target_pairs={{0,4},{1,5},{2,6},{3,7},{8,12},{9,13},{10,14},{11,15},{16,20},{17,... | collective-permute-start | bytes 245768 | tf_op jit(solution)/shard_map/ppermute | solution.py:50
  292.6 30.6 %collective-permute-start.4 = (bf16[1,640,64]{1,2,0:T(8,128)(2,1)S(1)}, bf16[1,640,64]{1,2,0:T(8,128)(2,1)S(1)}, u32[]{:S(2)}, u32[]{:S(2)}) collective-permute-start(bf16[1,640,64]{1,2,0:T(8,128)(2,1)S(1)} %get-tuple-element.104), channel_id=1, source_target_pairs={{4,0},{5,1},{6,2},{7,3},{12,8},{13,9},{14,10},{15,11},{20,16},{21,... | collective-permute-start | bytes 245768 | tf_op jit(solution)/shard_map/ppermute | solution.py:51
  323.9 2.2 copy-start.10
  324.1 2.8 copy-start.2
  326.9 13.6 %copy-start.3 = (f32[1024,640]{1,0:T(8,128)S(1)}, f32[1024,640]{1,0:T(8,128)}, u32[]{:S(2)}) copy-start(f32[1024,640]{1,0:T(8,128)} %copy-done.1) | copy-start | bytes 7864324
  349.9 3.5 copy-start.13
  349.9 3.5 copy-start.15
  349.9 3.5 copy-start.17
  349.9 3.5 copy-start.19
  381.6 47.8 %copy-start.7 = (f32[4,204800]{1,0:T(4,128)S(1)}, f32[4,204800]{1,0:T(4,128)}, u32[]{:S(2)}) copy-start(f32[4,204800]{1,0:T(4,128)} %reshape.1491) | copy-start | bytes 9830404
  429.4 17.3 %copy-start.21 = (f32[4,320]{1,0:T(4,128)S(1)}, f32[4,320]{1,0:T(4,128)}, u32[]{:S(2)}) copy-start(f32[4,320]{1,0:T(4,128)} %convert_reduce_fusion.3) | copy-start | bytes 15364
  472.1 157.5 %reduce-scatter.8.cloned.1.call-start = ((), (), s32[]{:S(2)}) async-start(), calls=%async_computation.9 | async-start | bytes 9256960 | tf_op jit(solution)/shard_map/reduce_scatter | solution.py:240
  497.1 170.1 %copy-start.20 = (f32[4,320]{1,0:T(4,128)S(1)}, f32[4,320]{1,0:T(4,128)}, u32[]{:S(2)}) copy-start(f32[4,320]{1,0:T(4,128)} %get-tuple-element.114) | copy-start | bytes 15364
  497.1 170.2 %copy-start.9 = (f32[1024,640]{1,0:T(8,128)S(1)}, f32[1024,640]{1,0:T(8,128)}, u32[]{:S(2)}) copy-start(f32[1024,640]{1,0:T(8,128)} %copy-done.8) | copy-start | bytes 7864324
  497.2 170.1 %reduce-scatter.10.cloned.1.call-start = ((), (), s32[]{:S(2)}) async-start(), calls=%async_computation.11 | async-start | bytes 2314240
  629.7 166.5 %all-gather.7.cloned.1.call-start = ((), (), s32[]{:S(2)}) async-start(), calls=%async_computation.10 | async-start | bytes 4165632 | tf_op jit(solution)/shard_map/all_gather | solution.py:242
  709.9 43.0 %all-to-all-start.1 = ((bf16[4,2,163840]{2,1,0:T(2,128)(2,1)}), bf16[4,2,163840]{2,1,0:T(2,128)(2,1)}, u32[]{:S(2)}, u32[]{:S(2)}) async-start(bf16[4,2,163840]{2,1,0:T(2,128)(2,1)} %reshape.1509), calls=%async_computation.1 | async-start | bytes 5242880 | tf_op jit(solution)/shard_map/all_to_all | solution.py:75
  752.8 34.5 %all-to-all-start.3 = ((bf16[4,2,163840]{2,1,0:T(2,128)(2,1)}), bf16[4,2,163840]{2,1,0:T(2,128)(2,1)S(1)}, u32[]{:S(2)}, u32[]{:S(2)}) async-start(bf16[4,2,163840]{2,1,0:T(2,128)(2,1)} %reshape.1511), calls=%async_computation.3 | async-start | bytes 5242880 | tf_op jit(solution)/shard_map/all_to_all | solution.py:75
Sparse Core Ops, SparseCore 0:
  13.4 131.5 all-gather.4
  472.3 24.8 reduce-scatter.5
  499.5 130.0 reduce-scatter.7
  632.5 34.6 reduce-scatter.9
  668.7 42.8 all-gather.6
where the time goes:
time: 824 us; the launch traced here: 816 us
  local copies, waits for them, and re-layouts  273 us (33%)
  waiting for transfers between devices  263 us (32%)
  matrix products  95.8 us (12%)
  other arithmetic  90.6 us (11%)
  blocking collectives  49.7 us (6%)
  starting transfers between devices  29.4 us (4%)
  between operations  14.6 us (2%)
    unnamed x88, local copies, waits for them, and re-layouts  160 us
    reduce_scatter x1, waiting for transfers between devices, local(): stack = lax.psum_scatter(stack, 'batch', scatter_dimension=1, tiled=True)  132 us
    all_gather x1, blocking collectives, local(): lax.all_gather(jnp.concatenate(smalls), 'ch', axis=0, tiled=False)  49.7 us
    all_gather x1, waiting for transfers between devices, local(): lax.all_gather(packed.reshape(1, -1, 128), 'ch', axis=0, tiled=True)  48.7 us
    unnamed x10, other arithmetic  46 us
    unnamed x6, waiting for transfers between devices  37.6 us
    reduce_scatter x1, waiting for transfers between devices, local(): stack = lax.psum_scatter(stack, 'seq', scatter_dimension=1, tiled=True)  24.9 us
    reshape x11, local copies, waits for them, and re-layouts, local(): flat = [g.reshape(nch, -1) for g in grads]  21.3 us
  transfers between devices with their start and end apart: 15, of which 5 were waited for; matrix products, arithmetic and copies ran while one was open for 28% of the time, Pallas kernels for 0%

commit v1 on v0

--- a/solution.py
+++ b/solution.py
@@ -6,6 +6,17 @@
 KERNEL_TAPS = 5
 DILATION_SPACING = 32
 EPSILON = 1e-05
+
+
+def split_up(x, dim, size):
+    before, after = (x.shape[:dim], x.shape[dim + 1 :])
+    return jnp.moveaxis(x.reshape(*before, size, -1, *after), dim, 0)
+
+
+def joined_along(pieces, dim):
+    pieces = jnp.moveaxis(pieces, 0, dim)
+    shape = pieces.shape
+    return pieces.reshape(*shape[:dim], shape[dim] * shape[dim + 1], *shape[dim + 2 :])
 
 
 def gelu_exact(values):
@@ -72,7 +83,14 @@
 
 
 def to_channels(x, nch, q_count, rows):
-    x = lax.all_to_all(x, "ch", 1, 0, tiled=True)
+    peers, position = (lax.axis_size("ch"), lax.axis_index("ch"))
+    blocks = split_up(x, 1, peers)
+    outs_2 = [blocks[position]]
+    for step in range(1, peers):
+        sent = blocks[position ^ step]
+        outs_2.append(lax.ppermute(sent, "ch", [(i_2, i_2 ^ step) for i_2 in range(peers)]))
+    blocks = jnp.stack(outs_2)[position ^ jnp.arange(peers)]
+    x = joined_along(blocks, 0)
     if q_count > 1:
         _, width, part = x.shape
         x = (

time: 824 us -> 780 us (0.947)
  local copies, waits for them, and re-layouts: 273 us -> 241 us
  other arithmetic: 90.6 us -> 61.7 us
  waiting for transfers between devices: 263 us -> 281 us
    ppermute x0 -> x6, waiting for transfers between devices: none -> 37.2 us  [to_channels(): lax.ppermute(sent, 'ch', [(i_2, i_2 ^ step) for i_2 in range(peers)])]
    unnamed x10 -> x8, other arithmetic: 46 us -> 14.9 us
    unnamed x88 -> x85, local copies, waits for them, and re-layouts: 160 us -> 133 us
    all_to_all x2 -> x0, waiting for transfers between devices: 19.7 us -> none  [to_channels(): x = lax.all_to_all(x, 'ch', 1, 0, tiled=True)]
    all_to_all x2 -> x0, starting transfers between devices: 8.88 us -> none  [to_channels(): x = lax.all_to_all(x, 'ch', 1, 0, tiled=True)]
    convert_element_type x1, local copies, waits for them, and re-layouts: 11.6 us -> 3.02 us  [local(): output = (residual + branch + b_out[:, None]).astype(jnp.bfloat16)]
  transfers between devices with their start and end apart: 15 -> 19, of which waited for: 5 -> 8; matrix products, arithmetic and copies ran while one was open for 28% -> 22% of each run, Pallas kernels for 0% -> 0%
where the time goes in v1:
time: 780 us; the launch traced here: 772 us
  waiting for transfers between devices  281 us (36%)
  local copies, waits for them, and re-layouts  241 us (31%)
  matrix products  95.8 us (12%)
  other arithmetic  61.7 us (8%)
  blocking collectives  49.7 us (6%)
  starting transfers between devices  28.2 us (4%)
  between operations  14.9 us (2%)
    unnamed x85, local copies, waits for them, and re-layouts  133 us
    reduce_scatter x1, waiting for transfers between devices, local(): stack = lax.psum_scatter(stack, 'batch', scatter_dimension=1, tiled=True)  132 us
    all_gather x1, blocking collectives, local(): lax.all_gather(jnp.concatenate(smalls), 'ch', axis=0, tiled=False)  49.7 us
    all_gather x1, waiting for transfers between devices, local(): lax.all_gather(packed.reshape(1, -1, 128), 'ch', axis=0, tiled=True)  48.7 us
    unnamed x6, waiting for transfers between devices  37.6 us
    ppermute x6, waiting for transfers between devices, to_channels(): lax.ppermute(sent, 'ch', [(i_2, i_2 ^ step) for i_2 in range(peers)])  37.2 us
    reduce_scatter x1, waiting for transfers between devices, local(): stack = lax.psum_scatter(stack, 'seq', scatter_dimension=1, tiled=True)  24.9 us
    reshape x11, local copies, waits for them, and re-layouts, local(): flat = [g.reshape(nch, -1) for g in grads]  21.3 us
  transfers between devices with their start and end apart: 19, of which 8 were waited for; matrix products, arithmetic and copies ran while one was open for 22% of the time, Pallas kernels for 0%

profile of v1, /device:TPU:0, one launch (start us, length us, event | category | flops | bytes accessed | tf_op | source)
XLA Modules:
  0.0 772.4 jit_solution(14650904212294518329)
XLA Ops:
  8.5 1.5 reshape.1483
  10.0 1.8 reshape.1482
  13.4 5.3 all-to-all-start
  22.4 49.7 %all-gather.1 = f32[4,1,1920]{2,1,0:T(1,128)S(1)} all-gather(f32[1,1,1920]{2,1,0:T(1,128)S(1)} %reshape.1540), channel_id=2, replica_groups=mesh['batch'=4,'seq'=2,'ch'=4] {'ch'}, dimensions={0}, use_global_device_ids=true | all-gather | bytes 38400 | tf_op jit(solution)/shard_map/all_gather | solution.py:149
  73.7 4.8 all-to-all-start.1
  81.5 14.8 %fusion.6 = bf16[1,1280,1,1,1,1,1024]{6,1,5,4,3,2,0:T(8,128)(2,1)} fusion(f32[1,1280,1,1,1,1,1024]{6,1,5,4,3,2,0:T(8,128)S(1)} %bitcast.302, f32[1280]{0:T(1024)S(1)} %add.178, f32[1280]{0:T(1024)S(1)} %mul.431, f32[1024]{0:T(1024)S(1)} %add_rsqrt_fusion.2, f32[1024]{0:T(1024)S(1)} %broadcast_multiply_fusion.8), kind=kLoop, calls=%fused_computation.13 | loop fusion | flops 90439680 | bytes 7882752 | tf_op jit(solution)/shard_map/convert_element_type | solution.py:182
  96.2 48.7 %all-gather.5.cloned.1.call-done = bf16[4,7200,128]{2,1,0:T(8,128)(2,1)} async-done(((bf16[1,7200,128]{2,1,0:T(8,128)(2,1)}), bf16[4,7200,128]{2,1,0:T(8,128)(2,1)}) %all-gather.5.cloned.1.call-update) | async-done | bytes 7372816 | tf_op jit(solution)/shard_map/all_gather | solution.py:158
  145.0 26.1 %copy.100 = bf16[1,4,7200,128]{3,1,2,0:T(4,128)(2,1)S(1)} copy(bf16[1,4,7200,128]{3,2,1,0:T(8,128)(2,1)} %bitcast.313) | data formatting | bytes 14745600
  171.1 3.0 copy-done.6
  174.0 2.0 fusion.111
  176.1 2.3 reshape.1486
  178.4 4.5 fusion.72
  183.5 7.3 multiply_convert_fusion.1
  191.8 1.9 collective-permute-start.1
  193.8 2.7 convert_reduce_fusion.3
  196.5 5.9 copy.71
  202.4 3.6 slice.216
  206.6 2.4 copy.70
  208.9 4.1 reshape.1490
  214.3 7.9 %copy.79 = bf16[5,640,640]{2,1,0:T(8,128)(2,1)} copy(bf16[5,640,640]{1,2,0:T(8,128)(2,1)} %bitcast.306) | data formatting | bytes 8192000 | tf_op jit(solution)/shard_map/transpose | solution.py:212
  222.2 2.9 fusion.90
  226.6 8.0 %constant_dynamic-update-slice_fusion = bf16[1,3200,1024]{1,2,0:T(8,128)(2,1)} fusion(bf16[1,3200,1024]{1,2,0:T(8,128)(2,1)} %fusion.99, f32[640]{0:T(1024)S(1)} %add.185, f32[640]{0:T(1024)S(1)} %mul.441, f32[1024]{0:T(1024)S(1)} %add_rsqrt_fusion.1, f32[1024]{0:T(1024)S(1)} %broadcast_multiply_fusion.5, f32[640]{0:T(1024)S(1)} %add.181, ...), kind=kLoop, calls=%fused_computation.200 | loop fusion | flops 45875200 | bytes 3948032
  237.5 9.6 %copy.85 = bf16[1,3200,1024]{2,1,0:T(8,128)(2,1)} copy(bf16[1,3200,1024]{1,2,0:T(8,128)(2,1)} %fusion.97) | data formatting | bytes 13107200 | tf_op jit(solution)/shard_map/concatenate | solution.py:74
  247.0 9.1 %fusion.74 = (f32[1024]{0:T(1024)S(1)}, f32[1024,640]{1,0:T(8,128)S(1)}) fusion(f32[640]{0:T(1024)S(1)} %add.188, bf16[3200,640]{1,0:T(8,128)(2,1)} %bitcast.307, bf16[1,3200,1024]{1,2,0:T(8,128)(2,1)} %fusion.97), kind=kOutput, calls=%fused_computation.150 | convolution fusion | flops 4195613696 | bytes 13277696 | tf_op jit(solution)/shard_map/co,rcl->rol/dot_general | solution.py:192
  256.7 11.8 %fusion.106 = f32[640,1280]{1,0:T(8,128)} fusion(bf16[1280,1024]{1,0:T(8,128)(2,1)} %bitcast.27, f32[640]{0:T(1024)S(1)} %add.192, f32[640]{0:T(1024)S(1)} %mul.451, f32[1024]{0:T(1024)S(1)} %add_rsqrt_fusion, f32[1024]{0:T(1024)S(1)} %broadcast_multiply_fusion.4, f32[640]{0:T(1024)S(1)} %add.188, f32[1024,640]{1,0:T(8,128)S(1)} %get-tuple-element.115), kind=kOutput, calls=%fused_computation.233 | convolution fusion | flops 1723596800 | bytes 8535552 | tf_op jit(solution)/shard_map/rhl,rdl->hd/dot_general | solution.py:200
  268.6 12.4 %fusion.50 = (f32[640]{0:T(1024)S(1)}, f32[1024]{0:T(1024)S(1)}, f32[1024]{0:T(1024)S(1)}, f32[640]{0:T(1024)S(1)}, f32[1,640,1024]{1,2,0:T(8,128)}) fusion(f32[1024]{0:T(1024)S(1)} %add_rsqrt_fusion, f32[1024]{0:T(1024)S(1)} %broadcast_multiply_fusion.4, f32[640]{0:T(1024)S(1)} %add.188, f32[1024,640]{1,0:T(8,128)S(1)} %get-tuple-element.115, ...), kind=kOutput, calls=%fused_computation.97 | convolution fusion | flops 1732113152 | bytes 9531904 | tf_op jit(solution)/shard_map/hd,rdl->rhl/dot_general | solution.py:201
  281.1 3.1 convert_reduce_fusion.1
  284.3 5.2 reshape.1509
  289.5 3.0 collective-permute-start.8
  293.9 7.6 convolution_bitcast_fusion
  301.5 9.7 %copy.87 = f32[640,5,640]{2,1,0:T(8,128)} copy(f32[640,5,640]{2,0,1:T(8,128)S(1)} %convolution_bitcast_fusion) | data formatting | bytes 16384000 | tf_op jit(solution)/shard_map/transpose | solution.py:240
  311.2 12.0 %reshape.1505 = f32[4,512000]{1,0:T(4,128)} reshape(f32[640,5,640]{2,1,0:T(8,128)} %copy.87) | data formatting | bytes 16384000 | tf_op jit(solution)/shard_map/reshape | solution.py:247
  326.9 13.5 %fusion.56 = (f32[640]{0:T(1024)S(1)}, f32[1024]{0:T(1024)S(1)}, f32[1024]{0:T(1024)S(1)}, f32[640]{0:T(1024)S(1)}, f32[1,640,1024]{1,2,0:T(8,128)}) fusion(f32[1024]{0:T(1024)S(1)} %add_rsqrt_fusion.1, f32[1024]{0:T(1024)S(1)} %broadcast_multiply_fusion.5, f32[640]{0:T(1024)S(1)} %add.181, f32[1024,640]{1,0:T(8,128)S(1)} %copy-done.2, f32[640]{0:T(1024)S(1)} %mul.441, ...), kind=kOutput, calls=%fused_computation.108 | convolution fusion | flops 4248695808 | bytes 15921664 | tf_op jit(solution)/shard_map/oc,rol->rcl/dot_general | solution.py:213
  340.5 3.3 convert_reduce_fusion.2
  343.9 6.0 fusion.57
  349.9 3.5 reshape.1500
  353.4 19.2 %multiply_reduce_fusion = (f32[1280]{0:T(1024)S(1)}, f32[1024]{0:T(1024)S(1)}, f32[1024]{0:T(1024)S(1)}, f32[1280]{0:T(1024)S(1)}, f32[1,1280,1024]{1,2,0:T(8,128)}) fusion(f32[1,1280,1024]{1,2,0:T(8,128)} %copy.71, f32[1024]{0:T(1024)S(1)} %copy-done.17, f32[1024]{0:T(1024)S(1)} %copy-done.19, f32[1280]{0:T(1024)S(1)} %copy-done.15, ...), kind=kOutput, calls=%fused_computation.26 | convolution fusion | flops 1785196032 | bytes 13471744 | tf_op jit(solution)/shard_map/dh,rhl->rdl/dot_general | solution.py:224
  375.6 1.8 constant_dynamic-update-slice_fusion.2
  381.6 43.2 %dynamic-update-slice.6 = f32[4,923520]{1,0:T(4,128)} dynamic-update-slice(f32[4,923520]{1,0:T(4,128)} %dynamic-update-slice.5, f32[4,512000]{1,0:T(4,128)} %reshape.1505, s32[]{} %constant.28, s32[]{} %constant.34) | dynamic-update-slice | bytes 16384004
  426.2 1.6 dynamic-update-slice.8
  429.2 17.2 %dynamic-update-slice.10 = f32[4,923520]{1,0:T(4,128)} dynamic-update-slice(f32[4,923520]{1,0:T(4,128)} %dynamic-update-slice.9, f32[4,204800]{1,0:T(4,128)S(1)} %copy-done.8, s32[]{} %constant.28, s32[]{} %constant.38) | dynamic-update-slice | bytes 6553604
  447.9 12.8 %pad_bitcast_fusion = f32[1,4,7232,128]{3,1,2,0:T(4,128)} fusion(f32[4,923520]{1,0:T(4,128)} %dynamic-update-slice.11), kind=kLoop, calls=%fused_computation.3 | loop fusion | bytes 29587456
  460.6 11.4 %copy.99 = f32[1,4,7232,128]{3,2,1,0:T(8,128)} copy(f32[1,4,7232,128]{3,1,2,0:T(4,128)} %pad_bitcast_fusion) | data formatting | bytes 29622272
  472.0 24.9 %reduce-scatter.6.cloned.1.call-done = f32[4,3616,128]{2,1,0:T(8,128)} async-done(((f32[4,7232,128]{2,1,0:T(8,128)}), f32[4,3616,128]{2,1,0:T(8,128)}) %reduce-scatter.6.cloned.1.call-update) | async-done | bytes 7405584 | tf_op jit(solution)/shard_map/reduce_scatter | solution.py:257
  497.0 132.5 %reduce-scatter.8.cloned.1.call-done = f32[4,904,128]{2,1,0:T(8,128)} async-done(((f32[4,3616,128]{2,1,0:T(8,128)}), f32[4,904,128]{2,1,0:T(8,128)}) %reduce-scatter.8.cloned.1.call-update) | async-done | bytes 1851408 | tf_op jit(solution)/shard_map/reduce_scatter | solution.py:258
  629.6 37.5 %reduce-scatter.10.cloned.1.call-done = f32[1,904,128]{2,1,0:T(8,128)} async-done(((f32[4,904,128]{2,1,0:T(8,128)}), f32[1,904,128]{2,1,0:T(8,128)}) %reduce-scatter.10.cloned.1.call-update) | async-done | bytes 462864
  667.2 5.1 copy.80
  672.3 11.7 %fusion.12 = bf16[1,1280,1024]{1,2,0:T(8,128)(2,1)} fusion(f32[1,1280,1024]{1,2,0:T(8,128)} %copy.71, bf16[640,1280]{1,0:T(8,128)(2,1)} %reshape.1490, f32[1280]{0:T(1024)S(1)} %add.196, f32[640]{0:T(1024)S(1)} %add.192, f32[640]{0:T(1024)S(1)} %mul.451, f32[1024]{0:T(1024)S(1)} %add_rsqrt_fusion, f32[1024]{0:T(1024)S(1)} %broadcast_multiply_fusion.4, ...), kind=kOutput, calls=%fused_computation.20 | convolution fusion | flops 1727528960 | bytes 12145152 | tf_op jit(solution)/shard_map/hd,rhl->rdl/dot_general | solution.py:197
  684.0 3.0 copy.72
  691.9 5.1 add_convert_fusion
  696.9 2.6 copy.81
  699.5 3.2 constant_dynamic-slice_fusion
  705.6 1.7 collective-permute-done.6
  708.6 12.7 %collective-permute-done.5 = bf16[1,320,1024]{2,1,0:T(8,128)(2,1)} collective-permute-done((bf16[1,320,1024]{2,1,0:T(8,128)(2,1)}, bf16[1,320,1024]{2,1,0:T(8,128)(2,1)}, u32[]{:S(2)}, u32[]{:S(2)}) %collective-permute-start.5) | collective-permute-done | bytes 655392 | tf_op jit(solution)/shard_map/ppermute | solution.py:91
  721.4 1.8 maximum_bitcast_fusion
  723.2 2.2 gather_fusion
  725.4 10.0 %collective-permute-done.11 = bf16[1,320,1024]{2,1,0:T(8,128)(2,1)} collective-permute-done((bf16[1,320,1024]{2,1,0:T(8,128)(2,1)}, bf16[1,320,1024]{2,1,0:T(8,128)(2,1)}, u32[]{:S(2)}, u32[]{:S(2)}) %collective-permute-start.11) | collective-permute-done | bytes 655392 | tf_op jit(solution)/shard_map/ppermute | solution.py:91
  735.4 12.8 %collective-permute-done.10 = bf16[1,320,1024]{2,1,0:T(8,128)(2,1)} collective-permute-done((bf16[1,320,1024]{2,1,0:T(8,128)(2,1)}, bf16[1,320,1024]{2,1,0:T(8,128)(2,1)}, u32[]{:S(2)}, u32[]{:S(2)}) %collective-permute-start.10) | collective-permute-done | bytes 655392 | tf_op jit(solution)/shard_map/ppermute | solution.py:91
  748.2 1.8 maximum_bitcast_fusion.1
  750.0 2.2 gather_fusion.1
  752.2 2.3 slice_bitcast_fusion
  756.1 1.9 slice.235
  761.3 2.4 reshape.1512
  763.7 1.7 copy.88
  (168 shorter events, 50.4 us)
Async XLA Ops:
  7.2 137.8 %all-gather.5.cloned.1.call-start = ((), (), s32[]{:S(2)}) async-start(), calls=%async_computation.5 | async-start | bytes 9216000 | tf_op jit(solution)/shard_map/all_gather | solution.py:158
  13.2 9.0 %copy-start.24 = (f32[320]{0:T(512)S(1)}, f32[320]{0:T(512)}, u32[]{:S(2)}) copy-start(f32[320]{0:T(512)} %param.17) | copy-start | bytes 3844
  13.3 9.0 %copy-start.25 = (f32[320]{0:T(512)S(1)}, f32[320]{0:T(512)}, u32[]{:S(2)}) copy-start(f32[320]{0:T(512)} %param.18) | copy-start | bytes 3844
  13.3 9.0 %copy-start.26 = (f32[320]{0:T(512)S(1)}, f32[320]{0:T(512)}, u32[]{:S(2)}) copy-start(f32[320]{0:T(512)} %param.28) | copy-start | bytes 3844
  13.3 9.0 %copy-start.27 = (f32[160]{0:T(256)S(1)}, f32[160]{0:T(256)}, u32[]{:S(2)}) copy-start(f32[160]{0:T(256)} %param.20) | copy-start | bytes 1924
  13.3 9.0 %copy-start.28 = (f32[160]{0:T(256)S(1)}, f32[160]{0:T(256)}, u32[]{:S(2)}) copy-start(f32[160]{0:T(256)} %param.21) | copy-start | bytes 1924
  13.3 9.0 %copy-start.29 = (f32[160]{0:T(256)S(1)}, f32[160]{0:T(256)}, u32[]{:S(2)}) copy-start(f32[160]{0:T(256)} %param.22) | copy-start | bytes 1924
  13.3 9.0 %copy-start.30 = (f32[160]{0:T(256)S(1)}, f32[160]{0:T(256)}, u32[]{:S(2)}) copy-start(f32[160]{0:T(256)} %param.24) | copy-start | bytes 1924
  13.3 9.0 %copy-start.31 = (f32[160]{0:T(256)S(1)}, f32[160]{0:T(256)}, u32[]{:S(2)}) copy-start(f32[160]{0:T(256)} %param.25) | copy-start | bytes 1924
  13.3 9.0 %copy-start.32 = (f32[160]{0:T(256)S(1)}, f32[160]{0:T(256)}, u32[]{:S(2)}) copy-start(f32[160]{0:T(256)} %param.26) | copy-start | bytes 1924
  13.4 60.4 %all-to-all-start = ((bf16[4,320,1024]{2,1,0:T(8,128)(2,1)}), bf16[4,320,1024]{2,1,0:T(8,128)(2,1)S(1)}, u32[]{:S(2)}, u32[]{:S(2)}) async-start(bf16[4,320,1024]{2,1,0:T(8,128)(2,1)} %param.15), calls=%async_computation | async-start | bytes 5242880 | tf_op jit(solution)/shard_map/all_to_all | solution.py:82
  19.5 54.1 %collective-permute-start = (s32[1,64]{1,0:T(1,128)S(1)}, s32[1,64]{1,0:T(1,128)S(1)}, u32[]{:S(2)}, u32[]{:S(2)}) collective-permute-start(s32[1,64]{1,0:T(1,128)S(1)} %get-tuple-element.110), channel_id=1, source_target_pairs={{0,4},{1,5},{2,6},{3,7},{8,12},{9,13},{10,14},{11,15},{16,20},{17,... | collective-permute-start | bytes 776 | tf_op jit(solution)/shard_map/ppermute | solution.py:61
  20.9 52.6 %collective-permute-start.2 = (s32[1,64]{1,0:T(1,128)S(1)}, s32[1,64]{1,0:T(1,128)S(1)}, u32[]{:S(2)}, u32[]{:S(2)}) collective-permute-start(s32[1,64]{1,0:T(1,128)S(1)} %get-tuple-element.111), channel_id=1, source_target_pairs={{4,0},{5,1},{6,2},{7,3},{12,8},{13,9},{14,10},{15,11},{20,16},{21,... | collective-permute-start | bytes 776 | tf_op jit(solution)/shard_map/ppermute | solution.py:62
  73.1 7.3 copy-start.14
  73.6 6.9 copy-start.20
  73.7 120.1 %all-to-all-start.1 = ((bf16[4,320,1024]{2,1,0:T(8,128)(2,1)}), bf16[4,320,1024]{2,1,0:T(8,128)(2,1)}, u32[]{:S(2)}, u32[]{:S(2)}) async-start(bf16[4,320,1024]{2,1,0:T(8,128)(2,1)} %param.29), calls=%async_computation.1 | async-start | bytes 5242880 | tf_op jit(solution)/shard_map/all_to_all | solution.py:82
  78.5 418.5 %reduce-scatter.6.cloned.1.call-start = ((), (), s32[]{:S(2)}) async-start(), calls=%async_computation.6 | async-start | bytes 22216704 | tf_op jit(solution)/shard_map/reduce_scatter | solution.py:257
  79.2 2.3 copy-start
  79.6 16.6 %copy-start.16 = (f32[1024]{0:T(1024)}, f32[1024]{0:T(1024)S(1)}, u32[]{:S(2)}) copy-start(f32[1024]{0:T(1024)S(1)} %broadcast_multiply_fusion.8) | copy-start | bytes 12292
  80.4 15.8 %copy-start.18 = (f32[1024]{0:T(1024)}, f32[1024]{0:T(1024)S(1)}, u32[]{:S(2)}) copy-start(f32[1024]{0:T(1024)S(1)} %add_rsqrt_fusion.2) | copy-start | bytes 12292
  171.0 3.0 copy-start.6
  182.9 43.7 %copy-start.1 = (f32[1024,640]{1,0:T(8,128)}, f32[1024,640]{1,0:T(8,128)S(1)}, u32[]{:S(2)}) copy-start(f32[1024,640]{1,0:T(8,128)S(1)} %get-tuple-element.113) | copy-start | bytes 7864324
  190.8 1.1 copy-start.4
  191.8 30.4 %collective-permute-start.1 = (bf16[1,640,64]{1,2,0:T(8,128)(2,1)S(1)}, bf16[1,640,64]{1,2,0:T(8,128)(2,1)S(1)}, u32[]{:S(2)}, u32[]{:S(2)}) collective-permute-start(bf16[1,640,64]{1,2,0:T(8,128)(2,1)S(1)} %get-tuple-element.100), channel_id=1, source_target_pairs={{0,4},{1,5},{2,6},{3,7},{8,12},{9,13},{10,14},{11,15},{16,20},{17,... | collective-permute-start | bytes 245768 | tf_op jit(solution)/shard_map/ppermute | solution.py:61
  213.1 21.5 %collective-permute-start.3 = (bf16[1,640,64]{1,2,0:T(8,128)(2,1)S(1)}, bf16[1,640,64]{1,2,0:T(8,128)(2,1)S(1)}, u32[]{:S(2)}, u32[]{:S(2)}) collective-permute-start(bf16[1,640,64]{1,2,0:T(8,128)(2,1)S(1)} %get-tuple-element.99), channel_id=1, source_target_pairs={{4,0},{5,1},{6,2},{7,3},{12,8},{13,9},{14,10},{15,11},{20,16},{21,... | collective-permute-start | bytes 245768 | tf_op jit(solution)/shard_map/ppermute | solution.py:62
  222.2 2.9 copy-start.5
  256.2 12.4 %copy-start.9 = (f32[1024,640]{1,0:T(8,128)}, f32[1024,640]{1,0:T(8,128)S(1)}, u32[]{:S(2)}) copy-start(f32[1024,640]{1,0:T(8,128)S(1)} %get-tuple-element.115) | copy-start | bytes 7864324
  256.7 11.8 %copy-start.13 = (bf16[640,1280]{1,0:T(8,128)(2,1)S(1)}, bf16[640,1280]{1,0:T(8,128)(2,1)}, u32[]{:S(2)}) copy-start(bf16[640,1280]{1,0:T(8,128)(2,1)} %reshape.1490) | copy-start | bytes 4915204
  289.5 34.6 %collective-permute-start.8 = (bf16[1,640,64]{1,2,0:T(8,128)(2,1)S(1)}, bf16[1,640,64]{1,2,0:T(8,128)(2,1)S(1)}, u32[]{:S(2)}, u32[]{:S(2)}) collective-permute-start(bf16[1,640,64]{1,2,0:T(8,128)(2,1)S(1)} %get-tuple-element.97), channel_id=1, source_target_pairs={{0,4},{1,5},{2,6},{3,7},{8,12},{9,13},{10,14},{11,15},{16,20},{17,... | collective-permute-start | bytes 245768 | tf_op jit(solution)/shard_map/ppermute | solution.py:61
  292.6 30.6 %collective-permute-start.7 = (bf16[1,640,64]{1,2,0:T(8,128)(2,1)S(1)}, bf16[1,640,64]{1,2,0:T(8,128)(2,1)S(1)}, u32[]{:S(2)}, u32[]{:S(2)}) collective-permute-start(bf16[1,640,64]{1,2,0:T(8,128)(2,1)S(1)} %get-tuple-element.98), channel_id=1, source_target_pairs={{4,0},{5,1},{6,2},{7,3},{12,8},{13,9},{14,10},{15,11},{20,16},{21,... | collective-permute-start | bytes 245768 | tf_op jit(solution)/shard_map/ppermute | solution.py:62
  323.9 2.2 copy-start.11
  324.1 2.8 copy-start.2
  326.9 13.6 %copy-start.3 = (f32[1024,640]{1,0:T(8,128)S(1)}, f32[1024,640]{1,0:T(8,128)}, u32[]{:S(2)}) copy-start(f32[1024,640]{1,0:T(8,128)} %copy-done.1) | copy-start | bytes 7864324
  349.9 3.5 copy-start.15
  349.9 3.5 copy-start.17
  349.9 3.5 copy-start.19
  349.9 3.5 copy-start.21
  381.6 47.6 %copy-start.8 = (f32[4,204800]{1,0:T(4,128)S(1)}, f32[4,204800]{1,0:T(4,128)}, u32[]{:S(2)}) copy-start(f32[4,204800]{1,0:T(4,128)} %reshape.1509) | copy-start | bytes 9830404
  429.2 17.3 %copy-start.23 = (f32[4,320]{1,0:T(4,128)S(1)}, f32[4,320]{1,0:T(4,128)}, u32[]{:S(2)}) copy-start(f32[4,320]{1,0:T(4,128)} %convert_reduce_fusion.3) | copy-start | bytes 15364
  472.0 157.5 %reduce-scatter.8.cloned.1.call-start = ((), (), s32[]{:S(2)}) async-start(), calls=%async_computation.7 | async-start | bytes 9256960 | tf_op jit(solution)/shard_map/reduce_scatter | solution.py:258
  497.0 170.2 %copy-start.22 = (f32[4,320]{1,0:T(4,128)S(1)}, f32[4,320]{1,0:T(4,128)}, u32[]{:S(2)}) copy-start(f32[4,320]{1,0:T(4,128)} %get-tuple-element.108) | copy-start | bytes 15364
  497.0 170.1 %reduce-scatter.10.cloned.1.call-start = ((), (), s32[]{:S(2)}) async-start(), calls=%async_computation.9 | async-start | bytes 2314240
  629.5 122.7 %all-gather.7.cloned.1.call-start = ((), (), s32[]{:S(2)}) async-start(), calls=%async_computation.8 | async-start | bytes 4165632 | tf_op jit(solution)/shard_map/all_gather | solution.py:260
  667.2 5.1 copy-start.10
  687.0 4.8 copy-start.7
  688.4 18.9 %collective-permute-start.6 = (bf16[1,320,1024]{2,1,0:T(8,128)(2,1)}, bf16[1,320,1024]{2,1,0:T(8,128)(2,1)}, u32[]{:S(2)}, u32[]{:S(2)}) collective-permute-start(bf16[1,320,1024]{2,1,0:T(8,128)(2,1)} %get-tuple-element.94), channel_id=1, source_target_pairs={{0,3},{1,2},{2,1},{3,0},{4,7},{5,6},{6,5},{7,4},{8,11},{9,10},{10,... | collective-permute-start | bytes 1966088 | tf_op jit(solution)/shard_map/ppermute | solution.py:91
  689.8 31.6 %collective-permute-start.5 = (bf16[1,320,1024]{2,1,0:T(8,128)(2,1)}, bf16[1,320,1024]{2,1,0:T(8,128)(2,1)}, u32[]{:S(2)}, u32[]{:S(2)}) collective-permute-start(bf16[1,320,1024]{2,1,0:T(8,128)(2,1)} %get-tuple-element.95), channel_id=1, source_target_pairs={{0,2},{1,3},{2,0},{3,1},{4,6},{5,7},{6,4},{7,5},{8,10},{9,11},{10,... | collective-permute-start | bytes 1966088 | tf_op jit(solution)/shard_map/ppermute | solution.py:91
  691.2 30.2 %collective-permute-start.4 = (bf16[1,320,1024]{2,1,0:T(8,128)(2,1)}, bf16[1,320,1024]{2,1,0:T(8,128)(2,1)}, u32[]{:S(2)}, u32[]{:S(2)}) collective-permute-start(bf16[1,320,1024]{2,1,0:T(8,128)(2,1)} %get-tuple-element.96), channel_id=1, source_target_pairs={{0,1},{1,0},{2,3},{3,2},{4,5},{5,4},{6,7},{7,6},{8,9},{9,8},{10,11... | collective-permute-start | bytes 1966088 | tf_op jit(solution)/shard_map/ppermute | solution.py:91
  702.8 32.6 %collective-permute-start.11 = (bf16[1,320,1024]{2,1,0:T(8,128)(2,1)}, bf16[1,320,1024]{2,1,0:T(8,128)(2,1)}, u32[]{:S(2)}, u32[]{:S(2)}) collective-permute-start(bf16[1,320,1024]{2,1,0:T(8,128)(2,1)} %get-tuple-element.90), channel_id=1, source_target_pairs={{0,3},{1,2},{2,1},{3,0},{4,7},{5,6},{6,5},{7,4},{8,11},{9,10},{10,... | collective-permute-start | bytes 1966088 | tf_op jit(solution)/shard_map/ppermute | solution.py:91
  704.2 43.9 %collective-permute-start.10 = (bf16[1,320,1024]{2,1,0:T(8,128)(2,1)}, bf16[1,320,1024]{2,1,0:T(8,128)(2,1)}, u32[]{:S(2)}, u32[]{:S(2)}) collective-permute-start(bf16[1,320,1024]{2,1,0:T(8,128)(2,1)} %get-tuple-element.91), channel_id=1, source_target_pairs={{0,2},{1,3},{2,0},{3,1},{4,6},{5,7},{6,4},{7,5},{8,10},{9,11},{10,... | collective-permute-start | bytes 1966088 | tf_op jit(solution)/shard_map/ppermute | solution.py:91
  707.2 41.0 %collective-permute-start.9 = (bf16[1,320,1024]{2,1,0:T(8,128)(2,1)}, bf16[1,320,1024]{2,1,0:T(8,128)(2,1)}, u32[]{:S(2)}, u32[]{:S(2)}) collective-permute-start(bf16[1,320,1024]{2,1,0:T(8,128)(2,1)} %get-tuple-element.92), channel_id=1, source_target_pairs={{0,1},{1,0},{2,3},{3,2},{4,5},{5,4},{6,7},{7,6},{8,9},{9,8},{10,11... | collective-permute-start | bytes 1966088 | tf_op jit(solution)/shard_map/ppermute | solution.py:91
  723.2 25.1 %copy-start.12 = (bf16[1,1,320,1024]{3,2,0,1:T(8,128)(2,1)S(1)}, bf16[1,1,320,1024]{3,2,0,1:T(8,128)(2,1)}, u32[]{:S(2)}) copy-start(bf16[1,1,320,1024]{3,2,0,1:T(8,128)(2,1)} %get-tuple-element.89) | copy-start | bytes 1966084
Sparse Core Ops, SparseCore 0:
  13.4 131.5 all-gather.4
  472.1 24.7 reduce-scatter.5
  499.4 130.0 reduce-scatter.7
  632.4 34.6 reduce-scatter.9
  668.5 42.8 all-gather.6
